TPU v7x, 32 devices: a whole 2x2x4 slice. The times are simulated.
32 devices in a mesh: dp: 8 (over y, x, core), tensor: 4 (over z).
Axes of the slice: x: 2, y: 2, z: 4, core: 2. Of those that a mesh axis runs over, the one named last changes fastest.
Arguments:
- teacher_hidden: bfloat16 [1024, 4096], P('dp'), may hold values from -6 to 6
- student_hidden: bfloat16 [1024, 2048], P('dp'), may hold values from -6 to 6
- target_ids: int32 [1024], P('dp'), may hold values from 0 to 64127
- teacher_head: bfloat16 [4096, 65536], P(None, ('dp', 'tensor')), may hold values from -1 to 1
- student_head: bfloat16 [2048, 65536], P(None, ('dp', 'tensor')), may hold values from -1 to 1
Outputs:
- head_grad: float32 [2048, 65536], P(None, ('dp', 'tensor'))
- input_grad: float32 [1024, 2048], P('dp', 'tensor')
All inputs are finite; a program needn't handle non-finite values.
Results may differ from a plain program's by a relative error of at most 0.0065.
Values may be sent and summed in bfloat16 or wider, within the bound.
A program may use at most 128 MiB of HBM per device.

v0:
```python
import jax
import jax.numpy as jnp
from jax import lax
from jax.sharding import PartitionSpec as P

VOCAB = 64128


def body(teacher_hidden, student_hidden, target_ids, teacher_head, student_head):
    width_cols = teacher_head.shape[1]
    first_col = (
        lax.axis_index("dp") * lax.axis_size("tensor") + lax.axis_index("tensor")
    ) * width_cols
    columns = first_col + lax.iota(jnp.int32, width_cols)
    is_real = (columns < VOCAB)[None, :]
    teacher_logits = jnp.dot(
        lax.all_gather(teacher_hidden, "dp", axis=0, tiled=True),
        teacher_head,
        preferred_element_type=jnp.float32,
    )
    teacher_logits = jnp.where(is_real, teacher_logits, jnp.float32(-1e30))
    student_rows, all_targets = (
        lax.all_gather(student_hidden, "dp", axis=0, tiled=True),
        lax.all_gather(target_ids, "dp", axis=0, tiled=True),
    )
    student_logits = jnp.where(
        is_real,
        jnp.dot(student_rows, student_head, preferred_element_type=jnp.float32),
        jnp.float32(-1e30),
    )
    teacher_peak, student_peak = lax.pmax(
        (jnp.max(teacher_logits, axis=1), jnp.max(student_logits, axis=1)), ("dp", "tensor")
    )
    teacher_expo = jnp.exp(teacher_logits - teacher_peak[:, None])
    student_expo = jnp.exp(student_logits - student_peak[:, None])
    teacher_total, student_total = lax.psum(
        (jnp.sum(teacher_expo, axis=1), jnp.sum(student_expo, axis=1)), ("dp", "tensor")
    )
    teacher_probs = teacher_expo / teacher_total[:, None]
    student_probs = student_expo / student_total[:, None]
    onehot = (all_targets[:, None] == columns[None, :]).astype(jnp.float32)
    logit_grad = (2.0 * student_probs - teacher_probs - onehot).astype(jnp.bfloat16)
    head_grad = lax.dot_general(
        student_rows, logit_grad, (((0,), (0,)), ((), ())), preferred_element_type=jnp.float32
    )
    own_rows = lax.psum_scatter(
        lax.dot_general(
            logit_grad, student_head, (((1,), (1,)), ((), ())), preferred_element_type=jnp.float32
        ),
        "dp",
        scatter_dimension=0,
        tiled=True,
    )
    input_grad = lax.psum_scatter(own_rows, "tensor", scatter_dimension=1, tiled=True)
    return (head_grad, input_grad)


def solution(mesh):
    placed = (
        P("dp", None),
        P("dp", None),
        P("dp"),
        P(None, ("dp", "tensor")),
        P(None, ("dp", "tensor")),
    )
    return jax.shard_map(
        body,
        mesh=mesh,
        in_specs=placed,
        out_specs=(P(None, ("dp", "tensor")), P("dp", "tensor")),
        check_vma=False,
    )
```

profile of v0, /device:TPU:0, one launch (start us, length us, event | category | flops | bytes accessed | tf_op | source)
XLA Modules:
  0.0 351.4 jit_solution(1641235967358725862)
XLA Ops:
  7.2 0.0 all-gather.4.cloned.1.call-start
  7.2 0.7 all-gather.4.cloned.1.call-update
  7.9 0.0 all-gather.6.cloned.1.call-start
  7.9 0.7 all-gather.6.cloned.1.call-update
  8.6 0.0 reduce-scatter.3.cloned.1.call-start
  8.7 10.4 %all-gather = s32[8,1,128]{2,1,0:T(1,128)S(1)} all-gather(s32[1,1,128]{2,1,0:T(1,128)} %bitcast.13), channel_id=1, replica_groups=mesh['dp'=8,'tensor'=4] {'dp'}, dimensions={0}, use_global_device_ids=true | all-gather | bytes 4608 | tf_op jit(solution)/shard_map/all_gather | solution.py:24
  19.1 30.1 %all-gather.4.cloned.1.call-done = bf16[1024,2048]{1,0:T(8,128)(2,1)} async-done(((bf16[128,2048]{1,0:T(8,128)(2,1)}), bf16[1024,2048]{1,0:T(8,128)(2,1)}) %all-gather.4.cloned.1.call-update) | async-done | bytes 4194320 | tf_op jit(solution)/shard_map/all_gather | solution.py:23
  49.2 14.5 %select_reduce_fusion.1 = (f32[1024]{0:T(1024)S(1)}, f32[1024,2048]{1,0:T(8,128)}) fusion(pred[2048]{0:T(1024)(128)(4,1)S(1)} %broadcast_compare_fusion, bf16[1024,2048]{1,0:T(8,128)(2,1)} %all-gather.4.cloned.1.call-done, bf16[2048,2048]{1,0:T(8,128)(2,1)} %param.9), kind=kOutput, calls=%fused_computation.5 | convolution fusion | flops 8594127872 | bytes 20977664 | tf_op jit(solution)/shard_map/dot_general | solution.py:28
  63.7 40.1 %pmax.14 = f32[1024]{0:T(1024)S(1)} all-reduce(f32[1024]{0:T(1024)S(1)} %get-tuple-element.10), channel_id=1, replica_groups=mesh['dp'=8,'tensor'=4] {'dp','tensor'}, use_global_device_ids=true, to_apply=%region_1.2 | all-reduce | flops 1024 | bytes 8192 | tf_op jit(solution)/shard_map/pmax | solution.py:31
  103.8 2.8 all-gather.6.cloned.1.call-done
  106.6 25.4 %fusion = (f32[1024]{0:T(1024)S(1)}, f32[1024]{0:T(1024)S(1)}, f32[1024,2048]{1,0:T(8,128)}) fusion(f32[1024,2048]{1,0:T(8,128)} %get-tuple-element.11, f32[1024]{0:T(1024)S(1)} %pmax.14, pred[2048]{0:T(1024)(128)(4,1)S(1)} %broadcast_compare_fusion, bf16[1024,4096]{1,0:T(8,128)(2,1)} %all-gather.6.cloned.1.call-done, bf16[4096,2048]{1,0:T(8,128)(2,1)} %param.8), kind=kOutput, calls=%fused_computation.6 | convolution fusion | flops 17190354944 | bytes 41957376 | tf_op jit(solution)/shard_map/dot_general | solution.py:16
  132.0 39.3 %pmax.15 = f32[1024]{0:T(1024)S(1)} all-reduce(f32[1024]{0:T(1024)S(1)} %get-tuple-element.7), channel_id=1, replica_groups=mesh['dp'=8,'tensor'=4] {'dp','tensor'}, use_global_device_ids=true, to_apply=%region_5.6 | all-reduce | flops 1024 | bytes 8192 | tf_op jit(solution)/shard_map/pmax | solution.py:31
  171.2 4.4 %fusion.1 = f32[1024]{0:T(1024)S(1)} fusion(f32[1024,2048]{1,0:T(8,128)} %get-tuple-element.12, f32[1024]{0:T(1024)S(1)} %pmax.15, pred[2048]{0:T(1024)(128)(4,1)S(1)} %broadcast_compare_fusion), kind=kLoop, calls=%fused_computation.7 | loop fusion | flops 6290432 | bytes 8398848 | tf_op jit(solution)/shard_map/reduce_sum | solution.py:37
  175.6 41.2 %all-reduce = (f32[1024]{0:T(1024)S(1)}, f32[1024]{0:T(1024)S(1)}) all-reduce(f32[1024]{0:T(1024)S(1)} %fusion.1, f32[1024]{0:T(1024)S(1)} %get-tuple-element.6), channel_id=1, replica_groups=mesh['dp'=8,'tensor'=4] {'dp','tensor'}, use_global_device_ids=true, to_apply=%region_7.8 | all-reduce | flops 2048 | bytes 16384 | tf_op jit(solution)/shard_map/psum | solution.py:36
  216.9 8.5 %subtract_convert_fusion = bf16[1024,2048]{1,0:T(8,128)(2,1)S(1)} fusion(f32[1024,2048]{1,0:T(8,128)} %get-tuple-element.11, f32[1024,2048]{1,0:T(8,128)} %get-tuple-element.12, s32[2048]{0:T(1024)S(1)} %iota_add_fusion, f32[1024]{0:T(1024)S(1)} %get-tuple-element.8, f32[1024]{0:T(1024)S(1)} %pmax.15, f32[1024]{0:T(1024)S(1)} %get-tuple-element.9, ...), kind=kLoop, calls=%fused_computation.1 | loop fusion | flops 25165824 | bytes 21002240 | tf_op jit(solution)/shard_map/convert_element_type | solution.py:42
  225.3 0.0 copy-start
  225.3 2.0 copy-done
  227.3 13.3 %fusion.2 = f32[1024,2048]{1,0:T(8,128)} fusion(bf16[1024,2048]{1,0:T(8,128)(2,1)S(1)} %subtract_convert_fusion, bf16[2048,2048]{1,0:T(8,128)(2,1)} %param.9), kind=kOutput, calls=%fused_computation.10 | convolution fusion | flops 8589934592 | bytes 20971520 | tf_op jit(solution)/shard_map/dot_general | solution.py:47
  240.6 0.0 reduce-scatter.3.cloned.1.call-update
  240.6 0.0 reduce-scatter.5.cloned.1.call-start
  240.6 71.4 %reduce-scatter.3.cloned.1.call-done = f32[128,2048]{1,0:T(8,128)} async-done(((f32[1024,2048]{1,0:T(8,128)}), f32[128,2048]{1,0:T(8,128)}) %reduce-scatter.3.cloned.1.call-update) | async-done | bytes 1048592 | tf_op jit(solution)/shard_map/reduce_scatter | solution.py:46
  312.0 0.0 reduce-scatter.5.cloned.1.call-update
  312.0 15.2 %convolution_bitcast_fusion = f32[2048,2048]{0,1:T(8,128)} fusion(bf16[1024,2048]{1,0:T(8,128)(2,1)} %copy-done, bf16[1024,2048]{1,0:T(8,128)(2,1)} %all-gather.4.cloned.1.call-done), kind=kOutput, calls=%fused_computation | convolution fusion | flops 8589934592 | bytes 25165824 | tf_op jit(solution)/shard_map/dot_general | solution.py:43
  327.2 17.6 %copy.8 = f32[2048,2048]{1,0:T(8,128)} copy(f32[2048,2048]{0,1:T(8,128)} %convolution_bitcast_fusion) | data formatting | bytes 33554432
  (3 shorter events, 0.0 us)
Async XLA Ops:
  7.2 42.0 %all-gather.4.cloned.1.call-start = ((), (), s32[]{:S(2)}) async-start(), calls=%async_computation.2 | async-start | bytes 4718592 | tf_op jit(solution)/shard_map/all_gather | solution.py:23
  7.9 98.7 %all-gather.6.cloned.1.call-start = ((), (), s32[]{:S(2)}) async-start(), calls=%async_computation.3 | async-start | bytes 9437184 | tf_op jit(solution)/shard_map/all_gather | solution.py:17
  8.6 303.4 %reduce-scatter.3.cloned.1.call-start = ((), (), s32[]{:S(2)}) async-start(), calls=%async_computation.4 | async-start | bytes 9437184 | tf_op jit(solution)/shard_map/reduce_scatter | solution.py:46
  225.3 2.0 copy-start
  240.6 104.3 %reduce-scatter.5.cloned.1.call-start = ((), (), s32[]{:S(2)}) async-start(), calls=%async_computation.5 | async-start | bytes 1310720 | tf_op jit(solution)/shard_map/reduce_scatter | solution.py:54
Sparse Core Ops, SparseCore 0:
  9.9 39.2 all-gather.3
  51.1 55.4 all-gather.5
  240.7 71.2 reduce-scatter.2
  314.7 27.2 reduce-scatter.4
where the time goes:
time: 352 us; the launch traced here: 351 us
  blocking collectives  131 us (37%)
  waiting for transfers between devices  106 us (30%)
  matrix products  68.4 us (19%)
  local copies, waits for them, and re-layouts  19.6 us (6%)
  between operations  13.8 us (4%)
  other arithmetic  12.8 us (4%)
    pmax x2, blocking collectives, body(): lax.pmax((jnp.max(teacher_logits, axis=1), jnp.max(student_logits, axis=1...  79.3 us
    reduce_scatter x1, waiting for transfers between devices, body(): lax.psum_scatter(lax.dot_general(logit_grad, student_head, (((1,), (1,)),...  71.4 us
    psum x1, blocking collectives, body(): lax.psum((jnp.sum(teacher_expo, axis=1), jnp.sum(student_expo, axis=1)),...  41.2 us
    all_gather x1, waiting for transfers between devices, body(): lax.all_gather(student_hidden, 'dp', axis=0, tiled=True)  30.1 us
    dot_general x1, matrix products, body(): jnp.dot(lax.all_gather(teacher_hidden, 'dp', axis=0, tiled=True), teacher...  25.4 us
    unnamed x3, local copies, waits for them, and re-layouts  19.6 us
    dot_general x1, matrix products, body(): lax.dot_general(student_rows, logit_grad, (((0,), (0,)), ((), ())), prefe...  15.2 us
    dot_general x1, matrix products, body(): jnp.dot(student_rows, student_head, preferred_element_type=jnp.float32)  14.5 us
  transfers between devices with their start and end apart: 4, of which 3 were waited for; matrix products, arithmetic and copies ran while one was open for 13% of the time, Pallas kernels for 0%

commit v1 on v0

--- a/solution.py
+++ b/solution.py
@@ -28,14 +28,18 @@
         jnp.dot(student_rows, student_head, preferred_element_type=jnp.float32),
         jnp.float32(-1e30),
     )
-    teacher_peak, student_peak = lax.pmax(
-        (jnp.max(teacher_logits, axis=1), jnp.max(student_logits, axis=1)), ("dp", "tensor")
+    peaks = jnp.stack([jnp.max(teacher_logits, axis=1), jnp.max(student_logits, axis=1)])
+    totals = jnp.stack(
+        [
+            jnp.sum(jnp.exp(teacher_logits - peaks[0][:, None]), axis=1),
+            jnp.sum(jnp.exp(student_logits - peaks[1][:, None]), axis=1),
+        ]
     )
-    teacher_expo = jnp.exp(teacher_logits - teacher_peak[:, None])
-    student_expo = jnp.exp(student_logits - student_peak[:, None])
-    teacher_total, student_total = lax.psum(
-        (jnp.sum(teacher_expo, axis=1), jnp.sum(student_expo, axis=1)), ("dp", "tensor")
-    )
+    table = lax.all_gather(jnp.concatenate([peaks, totals]), ("dp", "tensor"), axis=0)
+    top = jnp.max(table[:, :2], axis=0)
+    teacher_total, student_total = jnp.sum(table[:, 2:] * jnp.exp(table[:, :2] - top), axis=0)
+    teacher_expo = jnp.exp(teacher_logits - top[0][:, None])
+    student_expo = jnp.exp(student_logits - top[1][:, None])
     teacher_probs = teacher_expo / teacher_total[:, None]
     student_probs = student_expo / student_total[:, None]
     onehot = (all_targets[:, None] == columns[None, :]).astype(jnp.float32)

time: 352 us -> 334 us (0.949)
  blocking collectives: 131 us -> 82.3 us
  waiting for transfers between devices: 106 us -> 142 us
  other arithmetic: 12.8 us -> 8.64 us
    pmax x2 -> x0, blocking collectives: 79.3 us -> none  [body(): lax.pmax((jnp.max(teacher_logits, axis=1), jnp.max(student_logits, axis=1...]
    all_gather x0 -> x1, blocking collectives: none -> 71.9 us  [body(): lax.all_gather(jnp.concatenate([peaks, totals]), ('dp', 'tensor'), axis=0)]
    psum x1 -> x0, blocking collectives: 41.2 us -> none  [body(): lax.psum((jnp.sum(teacher_expo, axis=1), jnp.sum(student_expo, axis=1)),...]
    all_gather x1, waiting for transfers between devices: 2.8 us -> 41.7 us  [body(): lax.all_gather(teacher_hidden, 'dp', axis=0, tiled=True)]
    convert_element_type x1, other arithmetic: 8.47 us -> 4.86 us  [body(): (2.0 * student_probs - teacher_probs - onehot).astype(jnp.bfloat16)]
    unnamed x3 -> x5, local copies, waits for them, and re-layouts: 19.6 us -> 19.6 us
  transfers between devices with their start and end apart: 4 -> 4, of which waited for: 3 -> 3; matrix products, arithmetic and copies ran while one was open for 13% -> 14% of each run, Pallas kernels for 0% -> 0%
where the time goes in v1:
time: 334 us; the launch traced here: 333 us
  waiting for transfers between devices  142 us (43%)
  blocking collectives  82.3 us (25%)
  matrix products  66.8 us (20%)
  local copies, waits for them, and re-layouts  19.6 us (6%)
  between operations  13.8 us (4%)
  other arithmetic  8.64 us (3%)
    all_gather x1, blocking collectives, body(): lax.all_gather(jnp.concatenate([peaks, totals]), ('dp', 'tensor'), axis=0)  71.9 us
    reduce_scatter x1, waiting for transfers between devices, body(): lax.psum_scatter(lax.dot_general(logit_grad, student_head, (((1,), (1,)),...  68.7 us
    all_gather x1, waiting for transfers between devices, body(): lax.all_gather(teacher_hidden, 'dp', axis=0, tiled=True)  41.7 us
    all_gather x1, waiting for transfers between devices, body(): lax.all_gather(student_hidden, 'dp', axis=0, tiled=True)  30.1 us
    dot_general x1, matrix products, body(): jnp.dot(lax.all_gather(teacher_hidden, 'dp', axis=0, tiled=True), teacher...  23.9 us
    unnamed x5, local copies, waits for them, and re-layouts  19.6 us
    dot_general x1, matrix products, body(): lax.dot_general(student_rows, logit_grad, (((0,), (0,)), ((), ())), prefe...  15.2 us
    dot_general x1, matrix products, body(): jnp.dot(student_rows, student_head, preferred_element_type=jnp.float32)  14.5 us
  transfers between devices with their start and end apart: 4, of which 3 were waited for; matrix products, arithmetic and copies ran while one was open for 14% of the time, Pallas kernels for 0%

profile of v1, /device:TPU:0, one launch (start us, length us, event | category | flops | bytes accessed | tf_op | source)
XLA Modules:
  0.0 333.2 jit_solution(14643064451390198394)
XLA Ops:
  7.2 0.0 all-gather.6.cloned.1.call-start
  7.2 0.7 all-gather.6.cloned.1.call-update
  7.9 0.0 all-gather.8.cloned.1.call-start
  7.9 0.7 all-gather.8.cloned.1.call-update
  8.6 0.0 reduce-scatter.3.cloned.1.call-start
  8.7 10.4 %all-gather.2 = s32[8,1,128]{2,1,0:T(1,128)S(1)} all-gather(s32[1,1,128]{2,1,0:T(1,128)} %bitcast.31), channel_id=1, replica_groups=mesh['dp'=8,'tensor'=4] {'dp'}, dimensions={0}, use_global_device_ids=true | all-gather | bytes 4608 | tf_op jit(solution)/shard_map/all_gather | solution.py:24
  19.1 30.1 %all-gather.6.cloned.1.call-done = bf16[1024,2048]{1,0:T(8,128)(2,1)} async-done(((bf16[128,2048]{1,0:T(8,128)(2,1)}), bf16[1024,2048]{1,0:T(8,128)(2,1)}) %all-gather.6.cloned.1.call-update) | async-done | bytes 4194320 | tf_op jit(solution)/shard_map/all_gather | solution.py:23
  49.2 14.5 %fusion.3 = f32[1024,2048]{1,0:T(8,128)} fusion(bf16[1024,2048]{1,0:T(8,128)(2,1)} %all-gather.6.cloned.1.call-done, bf16[2048,2048]{1,0:T(8,128)(2,1)} %param.9), kind=kOutput, calls=%fused_computation.14 | convolution fusion | flops 8589934592 | bytes 20971520 | tf_op jit(solution)/shard_map/dot_general | solution.py:28
  63.7 41.7 %all-gather.8.cloned.1.call-done = bf16[1024,4096]{1,0:T(8,128)(2,1)} async-done(((bf16[128,4096]{1,0:T(8,128)(2,1)}), bf16[1024,4096]{1,0:T(8,128)(2,1)}) %all-gather.8.cloned.1.call-update) | async-done | bytes 8388624 | tf_op jit(solution)/shard_map/all_gather | solution.py:17
  105.4 23.9 %select_reduce_fusion = (f32[1024]{0:T(1024)S(1)}, f32[1024]{0:T(1024)S(1)}, f32[1024,2048]{1,0:T(8,128)S(1)}) fusion(pred[2048]{0:T(1024)(128)(4,1)S(1)} %broadcast_compare_fusion, f32[1024,2048]{1,0:T(8,128)} %fusion.3, bf16[1024,4096]{1,0:T(8,128)(2,1)} %all-gather.8.cloned.1.call-done, bf16[4096,2048]{1,0:T(8,128)(2,1)} %param.8), kind=kOutput, calls=%fused_computation.4 | convolution fusion | flops 17188257792 | bytes 41953280 | tf_op jit(solution)/shard_map/dot_general | solution.py:16
  129.3 0.0 copy-done
  129.3 3.4 %exponential_reduce_fusion.1 = (f32[1024]{0:T(1024)S(1)}, f32[1024]{0:T(1024)S(1)}) fusion(f32[1024,2048]{1,0:T(8,128)S(1)} %get-tuple-element.14, f32[1024]{0:T(1024)S(1)} %get-tuple-element.8, pred[2048]{0:T(1024)(128)(4,1)S(1)} %broadcast_compare_fusion, f32[1024]{0:T(1024)S(1)} %get-tuple-element.9, f32[1024,2048]{1,0:T(8,128)S(1)} %copy-done), kind=kLoop, calls=%fused_computation.3 | loop fusion | flops 12580864 | bytes 16795648 | tf_op jit(solution)/shard_map/reduce_sum | solution.py:34
  132.7 71.9 %all-gather.1 = f32[32,4,1024]{2,1,0:T(4,128)S(1)} all-gather(f32[1,4,1024]{2,1,0:T(4,128)S(1)} %maximum_bitcast_fusion), channel_id=2, replica_groups=mesh['dp'=8,'tensor'=4] {'dp','tensor'}, dimensions={0}, use_global_device_ids=true | all-gather | bytes 540672 | tf_op jit(solution)/shard_map/all_gather | solution.py:38
  204.6 0.1 slice_reduce_fusion
  204.7 0.3 fusion
  205.0 4.9 %subtract_convert_fusion = bf16[1024,2048]{1,0:T(8,128)(2,1)S(1)} fusion(f32[1024,2048]{1,0:T(8,128)S(1)} %get-tuple-element.14, f32[1024,2048]{1,0:T(8,128)S(1)} %copy-done, s32[2048]{0:T(1024)S(1)} %iota_add_fusion, f32[1024]{0:T(1024)S(1)} %bitcast.26, f32[1024]{0:T(1024)S(1)} %bitcast.24, f32[1024]{0:T(1024)S(1)} %bitcast.25, f32[1024]{0:T(1024)S(1)} %bitcast.23, ...), kind=kLoop, calls=%fused_computation.1 | loop fusion | flops 25165824 | bytes 21002240 | tf_op jit(solution)/shard_map/convert_element_type | solution.py:46
  209.9 2.0 copy-done.1
  211.8 13.3 %fusion.4 = f32[1024,2048]{1,0:T(8,128)} fusion(bf16[1024,2048]{1,0:T(8,128)(2,1)S(1)} %subtract_convert_fusion, bf16[2048,2048]{1,0:T(8,128)(2,1)} %param.9), kind=kOutput, calls=%fused_computation.15 | convolution fusion | flops 8589934592 | bytes 20971520 | tf_op jit(solution)/shard_map/dot_general | solution.py:51
  225.1 0.0 reduce-scatter.3.cloned.1.call-update
  225.1 0.0 reduce-scatter.5.cloned.1.call-start
  225.2 68.7 %reduce-scatter.3.cloned.1.call-done = f32[128,2048]{1,0:T(8,128)} async-done(((f32[1024,2048]{1,0:T(8,128)}), f32[128,2048]{1,0:T(8,128)}) %reduce-scatter.3.cloned.1.call-update) | async-done | bytes 1048592 | tf_op jit(solution)/shard_map/reduce_scatter | solution.py:50
  293.9 0.0 reduce-scatter.5.cloned.1.call-update
  293.9 15.2 %convolution_bitcast_fusion = f32[2048,2048]{0,1:T(8,128)} fusion(bf16[1024,2048]{1,0:T(8,128)(2,1)} %copy-done.1, bf16[1024,2048]{1,0:T(8,128)(2,1)} %all-gather.6.cloned.1.call-done), kind=kOutput, calls=%fused_computation | convolution fusion | flops 8589934592 | bytes 25165824 | tf_op jit(solution)/shard_map/dot_general | solution.py:47
  309.1 17.6 %copy.8 = f32[2048,2048]{1,0:T(8,128)} copy(f32[2048,2048]{0,1:T(8,128)} %convolution_bitcast_fusion) | data formatting | bytes 33554432
  (8 shorter events, 0.1 us)
Async XLA Ops:
  7.2 42.0 %all-gather.6.cloned.1.call-start = ((), (), s32[]{:S(2)}) async-start(), calls=%async_computation.2 | async-start | bytes 4718592 | tf_op jit(solution)/shard_map/all_gather | solution.py:23
  7.9 97.5 %all-gather.8.cloned.1.call-start = ((), (), s32[]{:S(2)}) async-start(), calls=%async_computation.3 | async-start | bytes 9437184 | tf_op jit(solution)/shard_map/all_gather | solution.py:17
  8.6 285.2 %reduce-scatter.3.cloned.1.call-start = ((), (), s32[]{:S(2)}) async-start(), calls=%async_computation.4 | async-start | bytes 9437184 | tf_op jit(solution)/shard_map/reduce_scatter | solution.py:50
  105.4 23.9 %copy-start = (f32[1024,2048]{1,0:T(8,128)S(1)}, f32[1024,2048]{1,0:T(8,128)}, u32[]{:S(2)}) copy-start(f32[1024,2048]{1,0:T(8,128)} %fusion.3) | copy-start | bytes 25165828
  209.9 2.0 copy-start.1
  225.1 101.6 %reduce-scatter.5.cloned.1.call-start = ((), (), s32[]{:S(2)}) async-start(), calls=%async_computation.5 | async-start | bytes 1310720 | tf_op jit(solution)/shard_map/reduce_scatter | solution.py:58
Sparse Core Ops, SparseCore 0:
  9.9 39.2 all-gather.5
  51.1 54.2 all-gather.7
  225.2 68.5 reduce-scatter.2
  296.6 27.3 reduce-scatter.4

commit v2 on v1

--- a/solution.py
+++ b/solution.py
@@ -1,6 +1,10 @@
+import functools
+
 import jax
 import jax.numpy as jnp
 from jax import lax
+from jax.experimental import pallas as pl
+from jax.experimental.pallas import tpu as pltpu
 from jax.sharding import PartitionSpec as P
 
 VOCAB = 64128
@@ -59,6 +63,339 @@
     return (head_grad, input_grad)
 
 
+MESH = pl.DeviceIdType.MESH
+LINKED = 9
+
+
+def as_column(row):
+    return jnp.transpose(jnp.broadcast_to(row, (row.shape[1], row.shape[1])))[:, :1]
+
+
+def as_row(column):
+    return jnp.transpose(jnp.broadcast_to(column, (column.shape[0], column.shape[0])))[:1, :]
+
+
+def kernel(
+    n, nt, tile,
+    teacher_in, student_in, ids_in, teacher_head, student_head,
+    grad_out, rows_out, input_out,
+    t_rows, s_rows, ids, t_w, s_w, t_exp, s_exp,
+    stats, local_peak, stats_in, scale, pair_in, plane_in, line_in,
+    local_sem, out_sem, gather_send, gather_recv, ids_send, ids_recv,
+    stats_send, stats_recv, pair_send, pair_recv, plane_send, plane_recv, line_send, line_recv,
+):
+    block = teacher_in.shape[0]
+    pair = 2 * block
+    width = t_w.shape[1]
+    depth = s_w.shape[0]
+    features = depth // nt
+    dp = lax.axis_index("dp")
+    tz = lax.axis_index("tensor")
+    chip, core = dp // 2, dp % 2
+
+    def flip(value, bit):
+        return value + bit - 2 * bit * ((value // bit) % 2)
+
+    def other(d):
+        out = chip
+        for bit in (1, 2):
+            if d & bit:
+                out = flip(out, bit)
+        return out
+
+    sibling = chip * 2 + 1 - core
+    near = (other(1) * 2 + core, other(2) * 2 + core)
+
+    barrier = pltpu.get_barrier_semaphore()
+    for k in range(1, n):
+        pl.semaphore_signal(barrier, inc=1, device_id=(lax.rem(dp + k, n), tz), device_id_type=MESH)
+    for k in range(1, nt):
+        pl.semaphore_signal(barrier, inc=1, device_id=(dp, lax.rem(tz + k, nt)), device_id_type=MESH)
+    pl.semaphore_wait(barrier, n - 1 + nt - 1)
+
+    def at(index, start=0, size=None):
+        return pl.ds(pl.multiple_of(index * block + start, block // 2), block if size is None else size)
+
+    def remote(source, target, send, recv, device):
+        return pltpu.make_async_remote_copy(
+            src_ref=source, dst_ref=target, send_sem=send, recv_sem=recv,
+            device_id=device, device_id_type=MESH,
+        )
+
+    def message(k, rows, device, from_input=False):
+        pieces = []
+        for a, (given, held) in enumerate(((student_in, s_rows), (teacher_in, t_rows))):
+            source = given if from_input else held.at[rows]
+            pieces.append(
+                remote(source, held.at[rows], gather_send.at[k, a], gather_recv.at[k, a], (device, tz))
+            )
+        return pieces
+
+    own = at(dp)
+    msgs = [message(0, own, sibling, True), message(1, own, near[0], True), message(2, own, near[1], True)]
+    for a in range(2):
+        for m in (msgs[1], msgs[2], msgs[0]):
+            m[a].start()
+    loads = [
+        pltpu.make_async_copy(student_in, s_rows.at[own], local_sem.at[0]),
+        pltpu.make_async_copy(student_head, s_w, local_sem.at[1]),
+        pltpu.make_async_copy(teacher_in, t_rows.at[own], local_sem.at[2]),
+        pltpu.make_async_copy(teacher_head, t_w, local_sem.at[3]),
+        pltpu.make_async_copy(ids_in, ids.at[dp], local_sem.at[4]),
+    ]
+    for load in loads:
+        load.start()
+    id_msgs = []
+    for k in range(1, n):
+        id_msgs.append(
+            remote(ids_in, ids.at[dp], ids_send.at[k - 1], ids_recv.at[k - 1], (lax.rem(dp + k, n), tz))
+        )
+        id_msgs[-1].start()
+
+    first_col = (dp * nt + tz) * width
+
+    def forward(which, d):
+        rows_ref, w_ref, exp_ref = ((s_rows, s_w, s_exp), (t_rows, t_w, t_exp))[which]
+        target = other(d)
+        rows = pl.ds(pl.multiple_of(target * pair, pair), pair)
+
+        def multiply(j, peak):
+            cols = pl.ds(pl.multiple_of(j * tile, tile), tile)
+            z = jnp.dot(rows_ref[rows, :], w_ref[:, cols], preferred_element_type=jnp.float32)
+            col = first_col + j * tile + lax.broadcasted_iota(jnp.int32, (1, tile), 1)
+            z = jnp.where(col < VOCAB, z, jnp.float32(-1e30))
+            exp_ref[rows, cols] = z
+            return jnp.maximum(peak, jnp.max(z, axis=1, keepdims=True))
+
+        peak = lax.fori_loop(0, width // tile, multiply, jnp.full((pair, 1), -jnp.inf, jnp.float32))
+
+        def exponential(j, total):
+            cols = pl.ds(pl.multiple_of(j * tile, tile), tile)
+            e = jnp.exp(exp_ref[rows, cols] - peak)
+            exp_ref[rows, cols] = e
+            return total + jnp.sum(e, axis=1, keepdims=True)
+
+        total = lax.fori_loop(0, width // tile, exponential, jnp.zeros((pair, 1), jnp.float32))
+        for h in range(2):
+            slot = pl.ds((1 - which) * n + target * 2 + h, 1)
+            stats[0, slot, :] = as_row(peak[h * block : (h + 1) * block])
+            stats[1, slot, :] = as_row(total[h * block : (h + 1) * block])
+
+    loads[0].wait()
+    loads[1].wait()
+    msgs[0][0].wait_recv()
+    forward(0, 0)
+    loads[2].wait()
+    loads[3].wait()
+    msgs[0][1].wait_recv()
+    forward(1, 0)
+
+    half = block // 2
+    across = other(3) * 2 + core
+    msgs.append(message(3, at(near[0], 0, half), near[1]))
+    msgs.append(message(4, at(near[1], half, half), near[0]))
+    msgs.append(message(5, at(near[0]), sibling))
+    msgs.append(message(6, at(near[1]), sibling))
+    msgs.append(message(7, at(across, 0, half), sibling))
+    msgs.append(message(8, at(across, half, half), sibling))
+    for a in range(2):
+        for k in (1, 2):
+            msgs[k][a].wait_recv()
+            msgs[k + 2][a].start()
+            msgs[k + 4][a].start()
+    for a in range(2):
+        msgs[5][a].wait_recv()
+        forward(a, 1)
+    msgs[6][0].wait_recv()
+    forward(0, 2)
+    for k in (3, 4):
+        msgs[k][0].wait_recv()
+        msgs[k + 4][0].start()
+    msgs[6][1].wait_recv()
+    forward(1, 2)
+    for k in (3, 4):
+        msgs[k][1].wait_recv()
+        msgs[k + 4][1].start()
+    for a in range(2):
+        msgs[7][a].wait_recv()
+        msgs[8][a].wait_recv()
+        forward(a, 3)
+    rows_copy = pltpu.make_async_copy(s_rows, rows_out, out_sem.at[4])
+    rows_copy.start()
+
+    local_peak[...] = stats[0]
+    partners = []
+    bit = 1
+    while bit < n:
+        partners.append((flip(dp, bit), tz))
+        bit *= 2
+    bit = 1
+    while bit < nt:
+        partners.append((dp, flip(tz, bit)))
+        bit *= 2
+    for r, partner in enumerate(partners):
+        swap = remote(stats, stats_in.at[r], stats_send.at[r], stats_recv.at[r], partner)
+        swap.start()
+        swap.wait()
+        mine, theirs = stats[0], stats_in[r, 0]
+        top = jnp.maximum(mine, theirs)
+        stats[1] = stats[1] * jnp.exp(mine - top) + stats_in[r, 1] * jnp.exp(theirs - top)
+        stats[0] = top
+    scale[...] = jnp.exp(local_peak[...] - stats[0]) / stats[1]
+    loads[4].wait()
+    for m in id_msgs:
+        m.wait()
+    for m in msgs:
+        for piece in m:
+            piece.wait_send()
+
+    tokens = t_rows.shape[0]
+    grads = t_w
+    outs, pairs, planes = [], {}, {}
+
+    def plane_rows(d):
+        return pl.ds(tokens + (d - 1) * block, block)
+
+    def reduce_pair(d):
+        pairs[d].wait()
+        mine = pl.ds(pl.multiple_of(other(d) * pair + core * block, block), block)
+        if d:
+            grads[plane_rows(d), :] = (t_exp[mine, :] + pair_in[d]).astype(jnp.bfloat16)
+            planes[d] = remote(
+                grads.at[plane_rows(d)], plane_in.at[d - 1],
+                plane_send.at[d - 1], plane_recv.at[d - 1], (other(d) * 2 + core, tz),
+            )
+            planes[d].start()
+
+    waiting = None
+    for d in (3, 1, 2, 0):
+        target = other(d)
+        rows = pl.ds(pl.multiple_of(target * pair, pair), pair)
+
+        def column_of(ref_row):
+            return jnp.concatenate([as_column(ref_row(h)) for h in range(2)], axis=0)
+
+        t_scale = column_of(lambda h: scale[pl.ds(target * 2 + h, 1), :])
+        s_scale = 2.0 * column_of(lambda h: scale[pl.ds(n + target * 2 + h, 1), :])
+        wanted = column_of(lambda h: ids[target * 2 + h][:1, :])
+
+        def gradient(j, carry):
+            cols = pl.ds(pl.multiple_of(j * tile, tile), tile)
+            col = (first_col + j * tile + lax.broadcasted_iota(jnp.int32, (1, tile), 1)).astype(jnp.float32)
+            g = s_exp[rows, cols] * s_scale - t_exp[rows, cols] * t_scale
+            g = g - jnp.where(wanted == col, 1.0, 0.0)
+            grads[rows, cols] = g.astype(jnp.bfloat16)
+            return carry
+
+        lax.fori_loop(0, width // tile, gradient, 0)
+        outs.append(pltpu.make_async_copy(grads.at[rows], grad_out.at[rows], out_sem.at[d]))
+        outs[-1].start()
+
+        def back(j, carry):
+            cols = pl.ds(pl.multiple_of(j * tile, tile), tile)
+            t_exp[rows, cols] = lax.dot_general(
+                grads[rows, :], s_w[cols, :], (((1,), (1,)), ((), ())), preferred_element_type=jnp.float32
+            )
+            return carry
+
+        lax.fori_loop(0, depth // tile, back, 0)
+        theirs = pl.ds(pl.multiple_of(target * pair + (1 - core) * block, block), block)
+        pairs[d] = remote(t_exp.at[theirs], pair_in.at[d], pair_send.at[d], pair_recv.at[d], (sibling, tz))
+        pairs[d].start()
+        if waiting is not None:
+            reduce_pair(waiting)
+        waiting = d
+    reduce_pair(0)
+    mine = pl.ds(pl.multiple_of(dp * block, block), block)
+    total = t_exp[mine, :] + pair_in[0]
+    for d in (1, 2, 3):
+        planes[d].wait()
+        total = total + plane_in[d - 1].astype(jnp.float32)
+    s_exp[0:block, :] = total
+    lines = []
+    for k in range(1, nt):
+        peer = lax.rem(tz + k, nt)
+        part = pl.ds(pl.multiple_of(peer * features, features), features)
+        lines.append(
+            remote(s_exp.at[0:block, part], line_in.at[k - 1], line_send.at[k - 1], line_recv.at[k - 1], (dp, peer))
+        )
+        lines[-1].start()
+    result = s_exp[0:block, pl.ds(pl.multiple_of(tz * features, features), features)]
+    for k in range(1, nt):
+        lines[k - 1].wait()
+        result = result + line_in[k - 1]
+    input_out[...] = result
+    for copy in outs:
+        copy.wait()
+    rows_copy.wait()
+
+
+def fused(n, nt, teacher_hidden, student_hidden, target_ids, teacher_head, student_head):
+    block, teacher_depth = teacher_hidden.shape
+    depth, width = student_head.shape
+    tokens = n * block
+    features = depth // nt
+    rounds = (n - 1).bit_length() + (nt - 1).bit_length()
+    ids = jnp.broadcast_to(target_ids.astype(jnp.float32)[None, :], (8, block))
+    f32, bf16, dma = jnp.float32, jnp.bfloat16, pltpu.SemaphoreType.DMA
+    anywhere = pl.BlockSpec(memory_space=pl.ANY)
+    whole = pl.BlockSpec(memory_space=pltpu.VMEM)
+    logit_grad, student_rows, input_grad = pl.pallas_call(
+        functools.partial(kernel, n, nt, min(512, width)),
+        out_shape=(
+            jax.ShapeDtypeStruct((tokens, width), bf16),
+            jax.ShapeDtypeStruct((tokens, depth), bf16),
+            jax.ShapeDtypeStruct((block, features), f32),
+        ),
+        in_specs=[anywhere, anywhere, whole, anywhere, anywhere],
+        out_specs=(anywhere, anywhere, whole),
+        scratch_shapes=[
+            pltpu.VMEM((tokens, teacher_depth), bf16),
+            pltpu.VMEM((tokens, depth), bf16),
+            pltpu.VMEM((n, 8, block), f32),
+            pltpu.VMEM((teacher_depth, width), bf16),
+            pltpu.VMEM((depth, width), bf16),
+            pltpu.VMEM((tokens, width), f32),
+            pltpu.VMEM((tokens, width), f32),
+            pltpu.VMEM((2, 2 * n, block), f32),
+            pltpu.VMEM((2 * n, block), f32),
+            pltpu.VMEM((rounds, 2, 2 * n, block), f32),
+            pltpu.VMEM((2 * n, block), f32),
+            pltpu.VMEM((n // 2, block, depth), f32),
+            pltpu.VMEM((n // 2 - 1, block, depth), bf16),
+            pltpu.VMEM((nt - 1, block, features), f32),
+            dma((5,)), dma((5,)),
+            dma((LINKED, 2)), dma((LINKED, 2)),
+            dma((n - 1,)), dma((n - 1,)),
+            dma((rounds,)), dma((rounds,)),
+            dma((n // 2,)), dma((n // 2,)),
+            dma((n // 2 - 1,)), dma((n // 2 - 1,)),
+            dma((nt - 1,)), dma((nt - 1,)),
+        ],
+        compiler_params=pltpu.CompilerParams(
+            collective_id=0, has_side_effects=True, vmem_limit_bytes=67043328
+        ),
+    )(teacher_hidden, student_hidden, ids, teacher_head, student_head)
+    head_grad = lax.dot_general(
+        student_rows, logit_grad, (((0,), (0,)), ((), ())), preferred_element_type=jnp.float32
+    )
+    return head_grad, input_grad
+
+
+def choose(n, nt, *arrays):
+    teacher_hidden, student_hidden, _, teacher_head, student_head = arrays
+    block, width = teacher_hidden.shape[0], student_head.shape[1]
+    fits = (
+        n == 8
+        and nt in (2, 4, 8)
+        and block == 128
+        and width == student_head.shape[0]
+        and width % 512 == 0
+        and teacher_head.shape[0] >= n * block + 3 * block
+    )
+    return fused(n, nt, *arrays) if fits else body(*arrays)
+
+
 def solution(mesh):
     placed = (
         P("dp", None),
@@ -68,7 +405,7 @@
         P(None, ("dp", "tensor")),
     )
     return jax.shard_map(
-        body,
+        functools.partial(choose, mesh.shape["dp"], mesh.shape["tensor"]),
         mesh=mesh,
         in_specs=placed,
         out_specs=(P(None, ("dp", "tensor")), P("dp", "tensor")),

time: 334 us -> 159 us (0.48)
  waiting for transfers between devices: 142 us -> 0 us
  Pallas kernels: 0 us -> 138 us
  blocking collectives: 82.3 us -> 0 us
  matrix products: 66.8 us -> 15.6 us
  local copies, waits for them, and re-layouts: 19.6 us -> 1.3 us
  between operations: 13.8 us -> 0.65 us
  other arithmetic: 8.64 us -> 0.66 us
    pallas_call x0 -> x1, Pallas kernels: none -> 138 us  [fused(): pl.pallas_call(functools.partial(kernel, n, nt, min(512, width)), out_sha...]
    all_gather x2 -> x0, blocking collectives: 82.3 us -> none  [the longest x1 71.9 us: body(): lax.all_gather(jnp.concatenate([peaks, totals]), ('dp', 'tensor'), axis=0)]
    all_gather x2 -> x0, waiting for transfers between devices: 71.8 us -> none  [the longest x1 41.7 us: body(): lax.all_gather(teacher_hidden, 'dp', axis=0, tiled=True)]
    reduce_scatter x2 -> x0, waiting for transfers between devices: 68.7 us -> none  [the longest x1 68.7 us: body(): lax.psum_scatter(lax.dot_general(logit_grad, student_head, (((1,), (1,)),...]
    dot_general x4 -> x1, matrix products: 66.8 us -> 15.6 us  [fused(): lax.dot_general(student_rows, logit_grad, (((0,), (0,)), ((), ())), prefe...]
    unnamed x5 -> x3, local copies, waits for them, and re-layouts: 19.6 us -> 0.71 us
    convert_element_type x1, other arithmetic: 4.86 us -> 0.66 us  [fused(): ids = jnp.broadcast_to(target_ids.astype(jnp.float32)[None, :], (8, block))]
    reduce_sum x2 -> x0, other arithmetic: 3.65 us -> none  [the longest x1 3.36 us: body(): jnp.sum(jnp.exp(teacher_logits - peaks[0][:, None]), axis=1)]
  transfers between devices with their start and end apart: 4 -> 0, of which waited for: 3 -> 0; matrix products, arithmetic and copies ran while one was open for 14% -> 0% of each run, Pallas kernels for 0% -> 0%
where the time goes in v2:
time: 159 us; the launch traced here: 156 us
  Pallas kernels  138 us (87%)
  matrix products  15.6 us (10%)
    pallas_call x1, Pallas kernels, fused(): pl.pallas_call(functools.partial(kernel, n, nt, min(512, width)), out_sha...  138 us
    dot_general x1, matrix products, fused(): lax.dot_general(student_rows, logit_grad, (((0,), (0,)), ((), ())), prefe...  15.6 us

profile of v2, /device:TPU:0, one launch (start us, length us, event | category | flops | bytes accessed | tf_op | source)
XLA Modules:
  0.0 156.1 jit_solution(14699331243735352280)
XLA Ops:
  0.6 0.7 convert_element_type.3
  1.3 0.6 broadcast_in_dim.2.ids_in
  1.9 137.9 %shard_map.68 = (bf16[1024,2048]{1,0:T(8,128)(2,1)}, bf16[1024,2048]{1,0:T(8,128)(2,1)}, f32[128,512]{1,0:T(8,128)}) custom-call(bf16[128,4096]{1,0:T(8,128)(2,1)} %teacher_in.1, bf16[128,2048]{1,0:T(8,128)(2,1)} %student_in.1, f32[8,128]{1,0:T(8,128)} %broadcast_in_dim.2.ids_in, bf16[4096,2048]{1,0:T(8,128)(2,1)} %teacher_head.1, ...), custom_call_target="tpu_custom_call" | custom-call | tf_op jit(solution)/shard_map/pallas_call | solution.py:343
  139.8 0.0 copy-start
  139.8 15.6 %fusion = f32[2048,2048]{1,0:T(8,128)} fusion(bf16[1024,2048]{1,0:T(8,128)(2,1)} %get-tuple-element.5, bf16[1024,2048]{1,0:T(8,128)(2,1)} %get-tuple-element.6), kind=kOutput, calls=%fused_computation | convolution fusion | flops 8589934592 | bytes 25165824 | tf_op jit(solution)/shard_map/dot_general | solution.py:379
  155.4 0.0 copy-done
  155.4 0.7 copy.8
Async XLA Ops:
  139.8 15.6 %copy-start = (f32[128,512]{1,0:T(8,128)S(1)}, f32[128,512]{1,0:T(8,128)}, u32[]{:S(2)}) copy-start(f32[128,512]{1,0:T(8,128)} %get-tuple-element.11) | copy-start | bytes 786436

commit v3 on v2

--- a/solution.py
+++ b/solution.py
@@ -78,12 +78,15 @@
 def kernel(
     n, nt, tile,
     teacher_in, student_in, ids_in, teacher_head, student_head,
-    grad_out, rows_out, input_out,
-    t_rows, s_rows, ids, t_w, s_w, t_exp, s_exp,
-    stats, local_peak, stats_in, scale, pair_in, plane_in, line_in,
-    local_sem, out_sem, gather_send, gather_recv, ids_send, ids_recv,
-    stats_send, stats_recv, pair_send, pair_recv, plane_send, plane_recv, line_send, line_recv,
+    grad_out, rows_out, *refs,
 ):
+    part_outs = refs[:nt]
+    (
+        t_rows, s_rows, ids, t_w, s_w, t_exp, s_exp,
+        stats, local_peak, stats_in, scale, pair_in, plane_in,
+        local_sem, out_sem, gather_send, gather_recv, ids_send, ids_recv,
+        stats_send, stats_recv, pair_send, pair_recv, plane_send, plane_recv,
+    ) = refs[nt:]
     block = teacher_in.shape[0]
     pair = 2 * block
     width = t_w.shape[1]
@@ -181,15 +184,6 @@
             stats[0, slot, :] = as_row(peak[h * block : (h + 1) * block])
             stats[1, slot, :] = as_row(total[h * block : (h + 1) * block])
 
-    loads[0].wait()
-    loads[1].wait()
-    msgs[0][0].wait_recv()
-    forward(0, 0)
-    loads[2].wait()
-    loads[3].wait()
-    msgs[0][1].wait_recv()
-    forward(1, 0)
-
     half = block // 2
     across = other(3) * 2 + core
     msgs.append(message(3, at(near[0], 0, half), near[1]))
@@ -198,28 +192,43 @@
     msgs.append(message(6, at(near[1]), sibling))
     msgs.append(message(7, at(across, 0, half), sibling))
     msgs.append(message(8, at(across, half, half), sibling))
-    for a in range(2):
+
+    def pass_on(a):
         for k in (1, 2):
             msgs[k][a].wait_recv()
             msgs[k + 2][a].start()
             msgs[k + 4][a].start()
-    for a in range(2):
-        msgs[5][a].wait_recv()
-        forward(a, 1)
-    msgs[6][0].wait_recv()
-    forward(0, 2)
-    for k in (3, 4):
-        msgs[k][0].wait_recv()
-        msgs[k + 4][0].start()
+
+    def pass_across(a):
+        for k in (3, 4):
+            msgs[k][a].wait_recv()
+            msgs[k + 4][a].start()
+
+    loads[0].wait()
+    loads[1].wait()
+    msgs[0][0].wait_recv()
+    forward(0, 0)
+    pass_on(0)
+    loads[2].wait()
+    loads[3].wait()
+    msgs[0][1].wait_recv()
+    forward(1, 0)
+    for d in (1, 2):
+        msgs[d + 4][0].wait_recv()
+        forward(0, d)
+    pass_on(1)
+    pass_across(0)
+    msgs[5][1].wait_recv()
+    forward(1, 1)
+    msgs[7][0].wait_recv()
+    msgs[8][0].wait_recv()
+    forward(0, 3)
     msgs[6][1].wait_recv()
+    pass_across(1)
     forward(1, 2)
-    for k in (3, 4):
-        msgs[k][1].wait_recv()
-        msgs[k + 4][1].start()
-    for a in range(2):
-        msgs[7][a].wait_recv()
-        msgs[8][a].wait_recv()
-        forward(a, 3)
+    msgs[7][1].wait_recv()
+    msgs[8][1].wait_recv()
+    forward(1, 3)
     rows_copy = pltpu.make_async_copy(s_rows, rows_out, out_sem.at[4])
     rows_copy.start()
 
@@ -312,19 +321,9 @@
         planes[d].wait()
         total = total + plane_in[d - 1].astype(jnp.float32)
     s_exp[0:block, :] = total
-    lines = []
-    for k in range(1, nt):
-        peer = lax.rem(tz + k, nt)
-        part = pl.ds(pl.multiple_of(peer * features, features), features)
-        lines.append(
-            remote(s_exp.at[0:block, part], line_in.at[k - 1], line_send.at[k - 1], line_recv.at[k - 1], (dp, peer))
-        )
-        lines[-1].start()
-    result = s_exp[0:block, pl.ds(pl.multiple_of(tz * features, features), features)]
-    for k in range(1, nt):
-        lines[k - 1].wait()
-        result = result + line_in[k - 1]
-    input_out[...] = result
+    for k in range(nt):
+        part = pl.ds(pl.multiple_of(lax.rem(tz + k, nt) * features, features), features)
+        part_outs[k][...] = s_exp[0:block, part]
     for copy in outs:
         copy.wait()
     rows_copy.wait()
@@ -340,15 +339,15 @@
     f32, bf16, dma = jnp.float32, jnp.bfloat16, pltpu.SemaphoreType.DMA
     anywhere = pl.BlockSpec(memory_space=pl.ANY)
     whole = pl.BlockSpec(memory_space=pltpu.VMEM)
-    logit_grad, student_rows, input_grad = pl.pallas_call(
+    logit_grad, student_rows, *parts = pl.pallas_call(
         functools.partial(kernel, n, nt, min(512, width)),
         out_shape=(
             jax.ShapeDtypeStruct((tokens, width), bf16),
             jax.ShapeDtypeStruct((tokens, depth), bf16),
-            jax.ShapeDtypeStruct((block, features), f32),
-        ),
+        )
+        + (jax.ShapeDtypeStruct((block, features), f32),) * nt,
         in_specs=[anywhere, anywhere, whole, anywhere, anywhere],
-        out_specs=(anywhere, anywhere, whole),
+        out_specs=(anywhere, anywhere) + (whole,) * nt,
         scratch_shapes=[
             pltpu.VMEM((tokens, teacher_depth), bf16),
             pltpu.VMEM((tokens, depth), bf16),
@@ -363,14 +362,12 @@
             pltpu.VMEM((2 * n, block), f32),
             pltpu.VMEM((n // 2, block, depth), f32),
             pltpu.VMEM((n // 2 - 1, block, depth), bf16),
-            pltpu.VMEM((nt - 1, block, features), f32),
             dma((5,)), dma((5,)),
             dma((LINKED, 2)), dma((LINKED, 2)),
             dma((n - 1,)), dma((n - 1,)),
             dma((rounds,)), dma((rounds,)),
             dma((n // 2,)), dma((n // 2,)),
             dma((n // 2 - 1,)), dma((n // 2 - 1,)),
-            dma((nt - 1,)), dma((nt - 1,)),
         ],
         compiler_params=pltpu.CompilerParams(
             collective_id=0, has_side_effects=True, vmem_limit_bytes=67043328
@@ -379,6 +376,10 @@
     head_grad = lax.dot_general(
         student_rows, logit_grad, (((0,), (0,)), ((), ())), preferred_element_type=jnp.float32
     )
+    input_grad = parts[0]
+    for k in range(1, nt):
+        ring = [(i, (i + k) % nt) for i in range(nt)]
+        input_grad = input_grad + lax.ppermute(parts[k], "tensor", ring)
     return head_grad, input_grad
 
 

time: 159 us -> 144 us (0.906)
  Pallas kernels: 138 us -> 118 us
  starting transfers between devices: 0 us -> 4.06 us
  waiting for transfers between devices: 0 us -> 1.7 us
    pallas_call x1, Pallas kernels: 138 us -> 118 us  [fused(): pl.pallas_call(functools.partial(kernel, n, nt, min(512, width)), out_sha...]
    ppermute x0 -> x3, starting transfers between devices: none -> 4.06 us  [fused(): input_grad = input_grad + lax.ppermute(parts[k], 'tensor', ring)]
    ppermute x0 -> x3, waiting for transfers between devices: none -> 1.7 us  [fused(): input_grad = input_grad + lax.ppermute(parts[k], 'tensor', ring)]
  transfers between devices with their start and end apart: 0 -> 3, of which waited for: 0 -> 1; matrix products, arithmetic and copies ran while one was open for 0% -> 11% of each run, Pallas kernels for 0% -> 0%
where the time goes in v3:
time: 144 us; the launch traced here: 141 us
  Pallas kernels  118 us (82%)
  matrix products  15.4 us (11%)
  starting transfers between devices  4.06 us (3%)
  waiting for transfers between devices  1.7 us (1%)
  other arithmetic  1.44 us (1%)
    pallas_call x1, Pallas kernels, fused(): pl.pallas_call(functools.partial(kernel, n, nt, min(512, width)), out_sha...  118 us
    dot_general x1, matrix products, fused(): lax.dot_general(student_rows, logit_grad, (((0,), (0,)), ((), ())), prefe...  15.4 us
    ppermute x3, starting transfers between devices, fused(): input_grad = input_grad + lax.ppermute(parts[k], 'tensor', ring)  4.06 us
  transfers between devices with their start and end apart: 3, of which 1 were waited for; matrix products, arithmetic and copies ran while one was open for 11% of the time, Pallas kernels for 0%

profile of v3, /device:TPU:0, one launch (start us, length us, event | category | flops | bytes accessed | tf_op | source)
XLA Modules:
  0.0 141.4 jit_solution(12563614519454233374)
XLA Ops:
  0.6 0.7 convert_element_type.3
  1.3 0.6 broadcast_in_dim.2.ids_in
  1.9 117.5 %shard_map.68 = (bf16[1024,2048]{1,0:T(8,128)(2,1)}, bf16[1024,2048]{1,0:T(8,128)(2,1)}, f32[128,512]{1,0:T(8,128)}, f32[128,512]{1,0:T(8,128)}, f32[128,512]{1,0:T(8,128)}, /*index=5*/f32[128,512]{1,0:T(8,128)}) custom-call(bf16[128,4096]{1,0:T(8,128)(2,1)} %teacher_in.1, bf16[128,2048]{1,0:T(8,128)(2,1)} %student_in.1, f32[8,128]{1,0:T(8,128)} %broadcast_in_dim.2.ids_in, ...), custom_call_target="tpu_custom_call" | custom-call | tf_op jit(solution)/shard_map/pallas_call | solution.py:342
  119.4 0.6 collective-permute-start
  120.1 2.0 %collective-permute-start.1 = (f32[128,512]{1,0:T(8,128)}, f32[128,512]{1,0:T(8,128)S(1)}, u32[]{:S(2)}, u32[]{:S(2)}) collective-permute-start(f32[128,512]{1,0:T(8,128)} %get-tuple-element.12), channel_id=1, source_target_pairs={{0,2},{1,3},{2,0},{3,1},{4,6},{5,7},{6,4},{7,5},{8,10},{9,11},{10,... | collective-permute-start | bytes 786440 | tf_op jit(solution)/shard_map/ppermute | solution.py:382
  122.1 1.4 collective-permute-start.2
  123.5 0.0 copy-start
  123.5 15.4 %fusion = f32[2048,2048]{1,0:T(8,128)} fusion(bf16[1024,2048]{1,0:T(8,128)(2,1)} %get-tuple-element.8, bf16[1024,2048]{1,0:T(8,128)(2,1)} %get-tuple-element.9), kind=kOutput, calls=%fused_computation.1 | convolution fusion | flops 8589934592 | bytes 25165824 | tf_op jit(solution)/shard_map/dot_general | solution.py:376
  138.9 0.0 collective-permute-done
  138.9 1.7 %collective-permute-done.1 = f32[128,512]{1,0:T(8,128)S(1)} collective-permute-done((f32[128,512]{1,0:T(8,128)}, f32[128,512]{1,0:T(8,128)S(1)}, u32[]{:S(2)}, u32[]{:S(2)}) %collective-permute-start.1) | collective-permute-done | bytes 262176 | tf_op jit(solution)/shard_map/ppermute | solution.py:382
  140.6 0.0 collective-permute-done.2
  140.6 0.0 copy-done
  140.6 0.8 add_add_fusion
Async XLA Ops:
  119.4 19.5 %collective-permute-start = (f32[128,512]{1,0:T(8,128)}, f32[128,512]{1,0:T(8,128)S(1)}, u32[]{:S(2)}, u32[]{:S(2)}) collective-permute-start(f32[128,512]{1,0:T(8,128)} %get-tuple-element.11), channel_id=1, source_target_pairs={{0,1},{1,2},{2,3},{3,0},{4,5},{5,6},{6,7},{7,4},{8,9},{9,10},{10,1... | collective-permute-start | bytes 786440 | tf_op jit(solution)/shard_map/ppermute | solution.py:382
  120.1 20.5 %collective-permute-start.1 = (f32[128,512]{1,0:T(8,128)}, f32[128,512]{1,0:T(8,128)S(1)}, u32[]{:S(2)}, u32[]{:S(2)}) collective-permute-start(f32[128,512]{1,0:T(8,128)} %get-tuple-element.12), channel_id=1, source_target_pairs={{0,2},{1,3},{2,0},{3,1},{4,6},{5,7},{6,4},{7,5},{8,10},{9,11},{10,... | collective-permute-start | bytes 786440 | tf_op jit(solution)/shard_map/ppermute | solution.py:382
  122.1 18.5 %collective-permute-start.2 = (f32[128,512]{1,0:T(8,128)}, f32[128,512]{1,0:T(8,128)S(1)}, u32[]{:S(2)}, u32[]{:S(2)}) collective-permute-start(f32[128,512]{1,0:T(8,128)} %get-tuple-element.13), channel_id=1, source_target_pairs={{0,3},{1,0},{2,1},{3,2},{4,7},{5,4},{6,5},{7,6},{8,11},{9,8},{10,9... | collective-permute-start | bytes 786440 | tf_op jit(solution)/shard_map/ppermute | solution.py:382
  123.5 17.1 %copy-start = (f32[128,512]{1,0:T(8,128)S(1)}, f32[128,512]{1,0:T(8,128)}, u32[]{:S(2)}) copy-start(f32[128,512]{1,0:T(8,128)} %get-tuple-element.10) | copy-start | bytes 786436
